TPU v7x, 256 devices: a whole 4x4x8 slice. The times are simulated.
256 devices in a mesh: section: 2 (over x_lo), ctx: 128 (over x_hi, y, z, core).
Axes of the slice: x: 4 (x_hi: 2, x_lo: 2; x = x_hi * 2 + x_lo), y: 4, z: 8, core: 2. Of those that a mesh axis runs over, the one named last changes fastest.
Arguments:
- query_rows: bfloat16 [2, 16384, 1536], P('section', 'ctx'), may hold values from -5 to 5
- key_rows: bfloat16 [2, 16384, 1536], P('section', 'ctx'), may hold values from -5 to 5
- value_rows: bfloat16 [2, 16384, 1536], P('section', 'ctx'), may hold values from -6 to 6
- grad_output: bfloat16 [2, 16384, 1536], P('section', 'ctx'), may hold values from -6 to 6
- block_lists: int32 [128, 5], P('ctx'), may hold values from -1 to 127, as said below
Outputs:
- grad_query: bfloat16 [2, 16384, 1536], P('section', 'ctx')
- grad_key: bfloat16 [2, 16384, 1536], P('section', 'ctx')
- grad_value: bfloat16 [2, 16384, 1536], P('section', 'ctx')
- handoff: bfloat16 [2, 16384, 1536], P('section', 'ctx')
Inputs may be any that keep to these rules, and one draw needn't show every extreme that they name: `block_lists`: each list names distinct key blocks whose devices lie within 2 devices of the query block's device, always including the query block itself; -1 marks an unused entry; in every draw some query block names all 5 blocks.
All inputs are finite; a program needn't handle non-finite values.
Results may differ from a plain program's by a relative error of at most 0.011.
Values may be sent and summed in bfloat16 or wider, within the bound.
A program may use at most 128 MiB of HBM per device.

v0:
```python
import jax
import jax.numpy as jnp
from jax import lax
from jax.sharding import PartitionSpec as P

H = 12
DH = 128
BLK = 128
REACH = 2


big_negative = -1e30


def from_behind(value, axis, steps):
    count = lax.axis_size(axis)
    first, last = (max(0, -steps), min(count, count - steps))
    return lax.ppermute(value, axis, [(source, source + steps) for source in range(first, last)])


def shortened(array):

    def short(part):
        return part.astype(jnp.bfloat16) if part.dtype == jnp.float32 else part

    return jax.tree.map(short, array)


def shards(query_rows, key_rows, value_rows, grad_output, block_lists):
    rows = query_rows.shape[1]
    width = query_rows.shape[2]
    per_device = block_lists.shape[0]
    scale = DH ** (-0.5)
    offsets = list(range(-REACH, REACH + 1))
    slab_count = len(offsets)
    position = lax.axis_index("ctx")
    own_query = query_rows[0].reshape(rows, H, DH)
    own_grad = grad_output[0].reshape(rows, H, DH)
    own_pair = jnp.stack([key_rows[0], value_rows[0]])
    fetched = {0: own_pair}
    lower = own_pair
    upper = own_pair
    for distance in range(1, REACH + 1):
        lower = from_behind(lower, "ctx", 1)
        upper = from_behind(upper, "ctx", -1)
        fetched[-distance] = lower
        fetched[distance] = upper
    slab_ids = jnp.stack(
        [(position + distance) * per_device + jnp.arange(per_device) for distance in offsets]
    )
    listed_ok = (block_lists >= 0)[:, :, None, None]
    needed = jnp.any(
        listed_ok & (block_lists[:, :, None, None] == slab_ids[None, None, :, :]), axis=1
    )
    row_needed = jnp.broadcast_to(
        needed[:, None, :, :, None], (per_device, BLK, slab_count, per_device, BLK)
    ).reshape(rows, slab_count * rows)
    every_pair = jnp.concatenate([fetched[distance] for distance in offsets], axis=1)
    keys_part = every_pair[0].reshape(-1, H, DH)
    scores = (
        jnp.einsum("qhd,khd->hqk", own_query, keys_part, preferred_element_type=jnp.float32) * scale
    )
    scores = jnp.where(row_needed[None], scores, big_negative)
    highest = jnp.max(scores, axis=2, keepdims=True)
    weights = jnp.exp(scores - highest)
    denom = jnp.sum(weights, axis=2, keepdims=True)
    probs = weights / denom
    probs_low = probs.astype(jnp.bfloat16)
    contribs = {}
    values_part = every_pair[1].reshape(-1, H, DH)
    attended = jnp.einsum(
        "hqk,khd->qhd", probs_low, values_part, preferred_element_type=jnp.float32
    )
    delta_heads = jnp.transpose(jnp.sum(own_grad.astype(jnp.float32) * attended, axis=2))
    keys_part = every_pair[0].reshape(-1, H, DH)
    values_part = every_pair[1].reshape(-1, H, DH)
    value_grad = jnp.einsum("hqk,qhd->khd", probs_low, own_grad, preferred_element_type=jnp.float32)
    grad_probs = jnp.einsum(
        "qhd,khd->hqk", own_grad, values_part, preferred_element_type=jnp.float32
    )
    grad_scores = probs * (grad_probs - delta_heads[:, :, None])
    scores_low = grad_scores.astype(jnp.bfloat16)
    query_grad = (
        jnp.einsum("hqk,khd->qhd", scores_low, keys_part, preferred_element_type=jnp.float32)
        * scale
    )
    key_grad = (
        jnp.einsum("hqk,qhd->khd", scores_low, own_query, preferred_element_type=jnp.float32)
        * scale
    )
    key_count = keys_part.shape[0]
    query_grad, terms_all = (
        query_grad,
        jnp.stack([key_grad.reshape(key_count, width), value_grad.reshape(key_count, width)]),
    )
    for index, distance in enumerate(offsets):
        contribs[distance] = terms_all[:, index * rows : (index + 1) * rows]
    upward = jnp.zeros((2, rows, width), jnp.float32)
    downward = jnp.zeros((2, rows, width), jnp.float32)
    for distance in range(REACH, 0, -1):
        upward = from_behind(shortened(upward + contribs[distance]), "ctx", 1)
        downward = from_behind(shortened(downward + contribs[-distance]), "ctx", -1)
    totals = contribs[0] + upward + downward
    grad_query = query_grad.reshape(rows, width).astype(jnp.bfloat16)[None]
    grad_key = totals[0].astype(jnp.bfloat16)[None]
    grad_value = totals[1].astype(jnp.bfloat16)[None]
    handoff = from_behind(grad_value, "section", -1)
    return (grad_query, grad_key, grad_value, handoff)


def solution(mesh):
    in_specs = (
        P("section", "ctx", None),
        P("section", "ctx", None),
        P("section", "ctx", None),
        P("section", "ctx", None),
        P("ctx", None),
    )
    out_specs = (
        P("section", "ctx", None),
        P("section", "ctx", None),
        P("section", "ctx", None),
        P("section", "ctx", None),
    )
    return jax.shard_map(shards, mesh=mesh, in_specs=in_specs, out_specs=out_specs, check_vma=False)
```

profile of v0, /device:TPU:4, one launch (start us, length us, event | category | flops | bytes accessed | tf_op | source)
XLA Modules:
  0.0 125.0 jit_solution(12889843022384734007)
XLA Ops:
  4.1 1.9 %collective-permute-start = (bf16[2,128,1536]{1,2,0:T(8,128)(2,1)}, bf16[2,128,1536]{1,2,0:T(8,128)(2,1)S(1)}, u32[]{:S(2)}, u32[]{:S(2)}) collective-permute-start(bf16[2,128,1536]{1,2,0:T(8,128)(2,1)} %pad_maximum_fusion.1), channel_id=1, source_target_pairs={{0,1},{1,2},{2,3},{3,4},{4,5},{5,6},{6,7},{7,8},{8,9},{9,10},{10,1... | collective-permute-start | bytes 2359304 | tf_op jit(solution)/shard_map/ppermute | solution.py:18
  6.0 9.6 %collective-permute-start.2 = (bf16[2,128,1536]{1,2,0:T(8,128)(2,1)}, bf16[2,128,1536]{1,2,0:T(8,128)(2,1)S(1)}, u32[]{:S(2)}, u32[]{:S(2)}) collective-permute-start(bf16[2,128,1536]{1,2,0:T(8,128)(2,1)} %pad_maximum_fusion.1), channel_id=1, source_target_pairs={{1,0},{2,1},{3,2},{4,3},{5,4},{6,5},{7,6},{8,7},{9,8},{10,9},{11,1... | collective-permute-start | bytes 2359304 | tf_op jit(solution)/shard_map/ppermute | solution.py:18
  15.6 7.9 %collective-permute-done = bf16[2,128,1536]{1,2,0:T(8,128)(2,1)S(1)} collective-permute-done((bf16[2,128,1536]{1,2,0:T(8,128)(2,1)}, bf16[2,128,1536]{1,2,0:T(8,128)(2,1)S(1)}, u32[]{:S(2)}, u32[]{:S(2)}) %collective-permute-start) | collective-permute-done | bytes 786464 | tf_op jit(solution)/shard_map/ppermute | solution.py:18
  23.6 1.9 %collective-permute-start.1 = (bf16[2,128,1536]{1,2,0:T(8,128)(2,1)S(1)}, bf16[2,128,1536]{1,2,0:T(8,128)(2,1)}, u32[]{:S(2)}, u32[]{:S(2)}) collective-permute-start(bf16[2,128,1536]{1,2,0:T(8,128)(2,1)S(1)} %collective-permute-done), channel_id=1, source_target_pairs={{0,1},{1,2},{2,3},{3,4},{4,5},{5,6},{6,7},{7,8},{8,9},{9,10},{10,1... | collective-permute-start | bytes 2359304 | tf_op jit(solution)/shard_map/ppermute | solution.py:18
  27.2 9.4 %collective-permute-start.3 = (bf16[2,128,1536]{1,2,0:T(8,128)(2,1)S(1)}, bf16[2,128,1536]{1,2,0:T(8,128)(2,1)S(1)}, u32[]{:S(2)}, u32[]{:S(2)}) collective-permute-start(bf16[2,128,1536]{1,2,0:T(8,128)(2,1)S(1)} %collective-permute-done.2), channel_id=1, source_target_pairs={{1,0},{2,1},{3,2},{4,3},{5,4},{6,5},{7,6},{8,7},{9,8},{10,9},{11,1... | collective-permute-start | bytes 2359304 | tf_op jit(solution)/shard_map/ppermute | solution.py:18
  36.6 6.1 %collective-permute-done.1 = bf16[2,128,1536]{1,2,0:T(8,128)(2,1)} collective-permute-done((bf16[2,128,1536]{1,2,0:T(8,128)(2,1)S(1)}, bf16[2,128,1536]{1,2,0:T(8,128)(2,1)}, u32[]{:S(2)}, u32[]{:S(2)}) %collective-permute-start.1) | collective-permute-done | bytes 786464 | tf_op jit(solution)/shard_map/ppermute | solution.py:18
  44.5 1.5 %collective-permute-done.3 = bf16[2,128,1536]{1,2,0:T(8,128)(2,1)S(1)} collective-permute-done((bf16[2,128,1536]{1,2,0:T(8,128)(2,1)S(1)}, bf16[2,128,1536]{1,2,0:T(8,128)(2,1)S(1)}, u32[]{:S(2)}, u32[]{:S(2)}) %collective-permute-start.3) | collective-permute-done | bytes 786464 | tf_op jit(solution)/shard_map/ppermute | solution.py:18
  46.3 1.7 %fusion.29 = (bf16[1,640,1536]{1,2,0:T(8,128)(2,1)}, bf16[1,640,1536]{1,2,0:T(8,128)(2,1)S(1)}) fusion(bf16[2,640,1536]{1,2,0:T(8,128)(2,1)S(1)} %constant_dynamic-update-slice_fusion), kind=kLoop, calls=%fused_computation.50 | loop fusion | bytes 7864320 | tf_op jit(solution)/shard_map/slice | solution.py:76
  48.0 3.5 %fusion.31 = (f32[12,128]{1,0:T(8,128)S(1)}, f32[12,128,640]{1,2,0:T(8,128)}) fusion(pred[640]{0:T(1024)(128)(4,1)S(1)} %broadcast_bitcast_fusion, bf16[640,12,128]{0,2,1:T(8,128)(2,1)S(1)} %bitcast.66, bf16[128,12,128]{0,2,1:T(8,128)(2,1)S(1)} %bitcast.70), kind=kOutput, calls=%fused_computation.52 | convolution fusion | flops 255591040 | bytes 6298240 | tf_op jit(solution)/shard_map/sub | solution.py:65
  51.5 2.5 %fusion.10 = bf16[12,128,640]{1,2,0:T(8,128)(2,1)S(1)} fusion(f32[12,128,640]{1,2,0:T(8,128)} %get-tuple-element.25, f32[12,128]{1,0:T(8,128)S(1)} %get-tuple-element.24), kind=kLoop, calls=%fused_computation.21 | loop fusion | flops 1966080 | bytes 5904384 | tf_op jit(solution)/shard_map/convert_element_type | solution.py:68
  54.1 2.9 %fusion.32 = f32[12,640,128]{1,2,0:T(8,128)} fusion(bf16[12,128,640]{1,2,0:T(8,128)(2,1)S(1)} %fusion.10, bf16[128,12,128]{0,2,1:T(8,128)(2,1)S(1)} %bitcast.72), kind=kOutput, calls=%fused_computation.53 | convolution fusion | flops 251658240 | bytes 6291456 | tf_op jit(solution)/shard_map/hqk,qhd->khd/dot_general | solution.py:77
  59.2 2.6 %multiply_bitcast_fusion = f32[640,12,128]{2,0,1:T(8,128)} fusion(bf16[12,128,640]{1,2,0:T(8,128)(2,1)S(1)} %fusion.2, bf16[128,12,128]{0,2,1:T(8,128)(2,1)S(1)} %bitcast.71), kind=kOutput, calls=%fused_computation.15 | convolution fusion | flops 252641280 | bytes 6291456 | tf_op jit(solution)/shard_map/hqk,qhd->khd/dot_general | solution.py:88
  61.8 5.5 %copy.52 = f32[640,12,128]{0,2,1:T(8,128)} copy(f32[640,12,128]{2,0,1:T(8,128)} %multiply_bitcast_fusion) | data formatting | bytes 7864320 | tf_op jit(solution)/shard_map/mul | solution.py:88
  67.3 4.0 %fusion.1 = bf16[2,640,1536]{1,2,0:T(8,128)(2,1)S(1)} fusion(f32[1,640,1536]{1,2,0:T(8,128)} %bitcast.60, f32[1,640,1536]{1,2,0:T(8,128)} %bitcast.63), kind=kLoop, calls=%fused_computation.8 | loop fusion | flops 1966080 | bytes 11796480 | tf_op jit(solution)/shard_map/convert.3
  71.5 2.1 %collective-permute-start.4 = (bf16[2,128,1536]{1,2,0:T(8,128)(2,1)S(1)}, bf16[2,128,1536]{1,2,0:T(8,128)(2,1)S(1)}, u32[]{:S(2)}, u32[]{:S(2)}) collective-permute-start(bf16[2,128,1536]{1,2,0:T(8,128)(2,1)S(1)} %get-tuple-element.18), channel_id=1, source_target_pairs={{0,1},{1,2},{2,3},{3,4},{4,5},{5,6},{6,7},{7,8},{8,9},{9,10},{10,1... | collective-permute-start | bytes 2359304 | tf_op jit(solution)/shard_map/ppermute | solution.py:18
  73.6 9.5 %collective-permute-start.6 = (bf16[2,128,1536]{1,2,0:T(8,128)(2,1)S(1)}, bf16[2,128,1536]{1,2,0:T(8,128)(2,1)S(1)}, u32[]{:S(2)}, u32[]{:S(2)}) collective-permute-start(bf16[2,128,1536]{1,2,0:T(8,128)(2,1)S(1)} %get-tuple-element.19), channel_id=1, source_target_pairs={{1,0},{2,1},{3,2},{4,3},{5,4},{6,5},{7,6},{8,7},{9,8},{10,9},{11,1... | collective-permute-start | bytes 2359304 | tf_op jit(solution)/shard_map/ppermute | solution.py:18
  83.1 7.7 %collective-permute-done.4 = bf16[2,128,1536]{1,2,0:T(8,128)(2,1)S(1)} collective-permute-done((bf16[2,128,1536]{1,2,0:T(8,128)(2,1)S(1)}, bf16[2,128,1536]{1,2,0:T(8,128)(2,1)S(1)}, u32[]{:S(2)}, u32[]{:S(2)}) %collective-permute-start.4) | collective-permute-done | bytes 786464 | tf_op jit(solution)/shard_map/ppermute | solution.py:18
  90.9 1.8 %collective-permute-done.6 = bf16[2,128,1536]{1,2,0:T(8,128)(2,1)S(1)} collective-permute-done((bf16[2,128,1536]{1,2,0:T(8,128)(2,1)S(1)}, bf16[2,128,1536]{1,2,0:T(8,128)(2,1)S(1)}, u32[]{:S(2)}, u32[]{:S(2)}) %collective-permute-start.6) | collective-permute-done | bytes 786464 | tf_op jit(solution)/shard_map/ppermute | solution.py:18
  93.0 1.9 %collective-permute-start.5 = (bf16[2,128,1536]{1,2,0:T(8,128)(2,1)S(1)}, bf16[2,128,1536]{1,2,0:T(8,128)(2,1)S(1)}, u32[]{:S(2)}, u32[]{:S(2)}) collective-permute-start(bf16[2,128,1536]{1,2,0:T(8,128)(2,1)S(1)} %get-tuple-element.16), channel_id=1, source_target_pairs={{0,1},{1,2},{2,3},{3,4},{4,5},{5,6},{6,7},{7,8},{8,9},{9,10},{10,1... | collective-permute-start | bytes 2359304 | tf_op jit(solution)/shard_map/ppermute | solution.py:18
  94.9 9.7 %collective-permute-start.7 = (bf16[2,128,1536]{1,2,0:T(8,128)(2,1)S(1)}, bf16[2,128,1536]{1,2,0:T(8,128)(2,1)S(1)}, u32[]{:S(2)}, u32[]{:S(2)}) collective-permute-start(bf16[2,128,1536]{1,2,0:T(8,128)(2,1)S(1)} %get-tuple-element.17), channel_id=1, source_target_pairs={{1,0},{2,1},{3,2},{4,3},{5,4},{6,5},{7,6},{8,7},{9,8},{10,9},{11,1... | collective-permute-start | bytes 2359304 | tf_op jit(solution)/shard_map/ppermute | solution.py:18
  104.6 7.6 %collective-permute-done.5 = bf16[2,128,1536]{1,2,0:T(8,128)(2,1)S(1)} collective-permute-done((bf16[2,128,1536]{1,2,0:T(8,128)(2,1)S(1)}, bf16[2,128,1536]{1,2,0:T(8,128)(2,1)S(1)}, u32[]{:S(2)}, u32[]{:S(2)}) %collective-permute-start.5) | collective-permute-done | bytes 786464 | tf_op jit(solution)/shard_map/ppermute | solution.py:18
  112.2 1.9 %collective-permute-done.7 = bf16[2,128,1536]{1,2,0:T(8,128)(2,1)S(1)} collective-permute-done((bf16[2,128,1536]{1,2,0:T(8,128)(2,1)S(1)}, bf16[2,128,1536]{1,2,0:T(8,128)(2,1)S(1)}, u32[]{:S(2)}, u32[]{:S(2)}) %collective-permute-start.7) | collective-permute-done | bytes 786464 | tf_op jit(solution)/shard_map/ppermute | solution.py:18
  114.4 1.3 %collective-permute-start.8 = (bf16[1,128,1536]{1,2,0:T(8,128)(2,1)S(1)}, bf16[1,128,1536]{1,2,0:T(8,128)(2,1)S(1)}, u32[]{:S(2)}, u32[]{:S(2)}) collective-permute-start(bf16[1,128,1536]{1,2,0:T(8,128)(2,1)S(1)} %get-tuple-element.22), channel_id=1, source_target_pairs={{128,0},{129,1},{130,2},{131,3},{132,4},{133,5},{134,6},{135,7},{1... | collective-permute-start | bytes 1179656 | tf_op jit(solution)/shard_map/ppermute | solution.py:18
  119.1 4.9 %collective-permute-done.8 = bf16[1,128,1536]{1,2,0:T(8,128)(2,1)S(1)} collective-permute-done((bf16[1,128,1536]{1,2,0:T(8,128)(2,1)S(1)}, bf16[1,128,1536]{1,2,0:T(8,128)(2,1)S(1)}, u32[]{:S(2)}, u32[]{:S(2)}) %collective-permute-start.8) | collective-permute-done | bytes 393248 | tf_op jit(solution)/shard_map/ppermute | solution.py:18
  (42 shorter events, 14.7 us)
Async XLA Ops:
  0.6 26.1 %copy-start.6 = (bf16[1,128,1536]{2,1,0:T(8,128)(2,1)S(1)}, bf16[1,128,1536]{2,1,0:T(8,128)(2,1)}, u32[]{:S(2)}) copy-start(bf16[1,128,1536]{2,1,0:T(8,128)(2,1)} %param.8) | copy-start | bytes 1179652
  0.6 26.4 %copy-start.7 = (s32[1,5]{1,0:T(1,128)S(1)}, s32[1,5]{1,0:T(1,128)}, u32[]{:S(2)}) copy-start(s32[1,5]{1,0:T(1,128)} %param.9) | copy-start | bytes 64
  4.1 19.5 %collective-permute-start = (bf16[2,128,1536]{1,2,0:T(8,128)(2,1)}, bf16[2,128,1536]{1,2,0:T(8,128)(2,1)S(1)}, u32[]{:S(2)}, u32[]{:S(2)}) collective-permute-start(bf16[2,128,1536]{1,2,0:T(8,128)(2,1)} %pad_maximum_fusion.1), channel_id=1, source_target_pairs={{0,1},{1,2},{2,3},{3,4},{4,5},{5,6},{6,7},{7,8},{8,9},{9,10},{10,1... | collective-permute-start | bytes 2359304 | tf_op jit(solution)/shard_map/ppermute | solution.py:18
  6.0 21.2 %collective-permute-start.2 = (bf16[2,128,1536]{1,2,0:T(8,128)(2,1)}, bf16[2,128,1536]{1,2,0:T(8,128)(2,1)S(1)}, u32[]{:S(2)}, u32[]{:S(2)}) collective-permute-start(bf16[2,128,1536]{1,2,0:T(8,128)(2,1)} %pad_maximum_fusion.1), channel_id=1, source_target_pairs={{1,0},{2,1},{3,2},{4,3},{5,4},{6,5},{7,6},{8,7},{9,8},{10,9},{11,1... | collective-permute-start | bytes 2359304 | tf_op jit(solution)/shard_map/ppermute | solution.py:18
  23.6 19.1 %collective-permute-start.1 = (bf16[2,128,1536]{1,2,0:T(8,128)(2,1)S(1)}, bf16[2,128,1536]{1,2,0:T(8,128)(2,1)}, u32[]{:S(2)}, u32[]{:S(2)}) collective-permute-start(bf16[2,128,1536]{1,2,0:T(8,128)(2,1)S(1)} %collective-permute-done), channel_id=1, source_target_pairs={{0,1},{1,2},{2,3},{3,4},{4,5},{5,6},{6,7},{7,8},{8,9},{9,10},{10,1... | collective-permute-start | bytes 2359304 | tf_op jit(solution)/shard_map/ppermute | solution.py:18
  27.2 18.9 %collective-permute-start.3 = (bf16[2,128,1536]{1,2,0:T(8,128)(2,1)S(1)}, bf16[2,128,1536]{1,2,0:T(8,128)(2,1)S(1)}, u32[]{:S(2)}, u32[]{:S(2)}) collective-permute-start(bf16[2,128,1536]{1,2,0:T(8,128)(2,1)S(1)} %collective-permute-done.2), channel_id=1, source_target_pairs={{1,0},{2,1},{3,2},{4,3},{5,4},{6,5},{7,6},{8,7},{9,8},{10,9},{11,1... | collective-permute-start | bytes 2359304 | tf_op jit(solution)/shard_map/ppermute | solution.py:18
  48.0 3.6 %copy-start.2 = (bf16[1,640,1536]{1,2,0:T(8,128)(2,1)}, bf16[1,640,1536]{1,2,0:T(8,128)(2,1)S(1)}, u32[]{:S(2)}) copy-start(bf16[1,640,1536]{1,2,0:T(8,128)(2,1)S(1)} %get-tuple-element.21) | copy-start | bytes 5898244
  54.1 2.9 %copy-start.5 = (bf16[1,640,1536]{1,2,0:T(8,128)(2,1)S(1)}, bf16[1,640,1536]{1,2,0:T(8,128)(2,1)}, u32[]{:S(2)}) copy-start(bf16[1,640,1536]{1,2,0:T(8,128)(2,1)} %get-tuple-element.20) | copy-start | bytes 5898244
  54.1 4.1 %copy-start.4 = (f32[12,128,640]{1,2,0:T(8,128)S(1)}, f32[12,128,640]{1,2,0:T(8,128)}, u32[]{:S(2)}) copy-start(f32[12,128,640]{1,2,0:T(8,128)} %get-tuple-element.25) | copy-start | bytes 11796484
  67.3 25.4 %copy-start = (f32[12,640,128]{1,2,0:T(8,128)S(1)}, f32[12,640,128]{1,2,0:T(8,128)}, u32[]{:S(2)}) copy-start(f32[12,640,128]{1,2,0:T(8,128)} %fusion.32) | copy-start | bytes 11796484
  67.3 25.4 %copy-start.1 = (f32[640,12,128]{0,2,1:T(8,128)S(1)}, f32[640,12,128]{0,2,1:T(8,128)}, u32[]{:S(2)}) copy-start(f32[640,12,128]{0,2,1:T(8,128)} %copy.52) | copy-start | bytes 11796484
  71.5 19.3 %collective-permute-start.4 = (bf16[2,128,1536]{1,2,0:T(8,128)(2,1)S(1)}, bf16[2,128,1536]{1,2,0:T(8,128)(2,1)S(1)}, u32[]{:S(2)}, u32[]{:S(2)}) collective-permute-start(bf16[2,128,1536]{1,2,0:T(8,128)(2,1)S(1)} %get-tuple-element.18), channel_id=1, source_target_pairs={{0,1},{1,2},{2,3},{3,4},{4,5},{5,6},{6,7},{7,8},{8,9},{9,10},{10,1... | collective-permute-start | bytes 2359304 | tf_op jit(solution)/shard_map/ppermute | solution.py:18
  73.6 19.0 %collective-permute-start.6 = (bf16[2,128,1536]{1,2,0:T(8,128)(2,1)S(1)}, bf16[2,128,1536]{1,2,0:T(8,128)(2,1)S(1)}, u32[]{:S(2)}, u32[]{:S(2)}) collective-permute-start(bf16[2,128,1536]{1,2,0:T(8,128)(2,1)S(1)} %get-tuple-element.19), channel_id=1, source_target_pairs={{1,0},{2,1},{3,2},{4,3},{5,4},{6,5},{7,6},{8,7},{9,8},{10,9},{11,1... | collective-permute-start | bytes 2359304 | tf_op jit(solution)/shard_map/ppermute | solution.py:18
  93.0 19.2 %collective-permute-start.5 = (bf16[2,128,1536]{1,2,0:T(8,128)(2,1)S(1)}, bf16[2,128,1536]{1,2,0:T(8,128)(2,1)S(1)}, u32[]{:S(2)}, u32[]{:S(2)}) collective-permute-start(bf16[2,128,1536]{1,2,0:T(8,128)(2,1)S(1)} %get-tuple-element.16), channel_id=1, source_target_pairs={{0,1},{1,2},{2,3},{3,4},{4,5},{5,6},{6,7},{7,8},{8,9},{9,10},{10,1... | collective-permute-start | bytes 2359304 | tf_op jit(solution)/shard_map/ppermute | solution.py:18
  94.9 20.8 %copy-start.3 = (bf16[1,640,1536]{1,2,0:T(8,128)(2,1)S(1)}, bf16[1,640,1536]{1,2,0:T(8,128)(2,1)}, u32[]{:S(2)}) copy-start(bf16[1,640,1536]{1,2,0:T(8,128)(2,1)} %copy-done.2) | copy-start | bytes 5898244
  94.9 19.2 %collective-permute-start.7 = (bf16[2,128,1536]{1,2,0:T(8,128)(2,1)S(1)}, bf16[2,128,1536]{1,2,0:T(8,128)(2,1)S(1)}, u32[]{:S(2)}, u32[]{:S(2)}) collective-permute-start(bf16[2,128,1536]{1,2,0:T(8,128)(2,1)S(1)} %get-tuple-element.17), channel_id=1, source_target_pairs={{1,0},{2,1},{3,2},{4,3},{5,4},{6,5},{7,6},{8,7},{9,8},{10,9},{11,1... | collective-permute-start | bytes 2359304 | tf_op jit(solution)/shard_map/ppermute | solution.py:18
  114.4 9.7 %collective-permute-start.8 = (bf16[1,128,1536]{1,2,0:T(8,128)(2,1)S(1)}, bf16[1,128,1536]{1,2,0:T(8,128)(2,1)S(1)}, u32[]{:S(2)}, u32[]{:S(2)}) collective-permute-start(bf16[1,128,1536]{1,2,0:T(8,128)(2,1)S(1)} %get-tuple-element.22), channel_id=1, source_target_pairs={{128,0},{129,1},{130,2},{131,3},{132,4},{133,5},{134,6},{135,7},{1... | collective-permute-start | bytes 1179656 | tf_op jit(solution)/shard_map/ppermute | solution.py:18
where the time goes:
time: 126 us; the launch traced here: 125 us
  starting transfers between devices  47.2 us (37%)
  waiting for transfers between devices  39.4 us (31%)
  local copies, waits for them, and re-layouts  17.7 us (14%)
  matrix products  11.4 us (9%)
  other arithmetic  8.31 us (7%)
    ppermute x9, starting transfers between devices, from_behind(): lax.ppermute(value, axis, [(source, source + steps) for source in range(f...  47.2 us
    ppermute x9, waiting for transfers between devices, from_behind(): lax.ppermute(value, axis, [(source, source + steps) for source in range(f...  39.4 us
    unnamed x27, local copies, waits for them, and re-layouts  9.83 us
    mul x1, local copies, waits for them, and re-layouts, shards(): jnp.einsum('hqk,qhd->khd', scores_low, own_query, preferred_element_type=...  5.45 us
    another operation x2, other arithmetic  4.25 us
    sub x1, matrix products, shards(): weights = jnp.exp(scores - highest)  3.55 us
    dot_general x1, matrix products, shards(): jnp.einsum('hqk,qhd->khd', probs_low, own_grad, preferred_element_type=jn...  2.85 us
    dot_general x1, matrix products, shards(): jnp.einsum('hqk,qhd->khd', scores_low, own_query, preferred_element_type=...  2.64 us
  transfers between devices with their start and end apart: 9, of which 8 were waited for; matrix products, arithmetic and copies ran while one was open for 6% of the time, Pallas kernels for 0%

commit v1 on v0

v1 whole, which is shorter than its diff:
```python
import functools

import jax
import jax.numpy as jnp
from jax import lax
from jax.experimental import pallas as pl
from jax.experimental.pallas import tpu as pltpu
from jax.sharding import PartitionSpec as P

H = 12
DH = 128
BLK = 128
REACH = 2
CORES = 2
SLOTS = H // CORES
ROWS = CORES * BLK
NEG = -1e30
MESH = pl.DeviceIdType.MESH
AHEAD = 2


def nt(a, b):
    return lax.dot_general(a, b, (((1,), (1,)), ((), ())), preferred_element_type=jnp.float32)


def nn(a, b):
    return lax.dot_general(a, b, (((1,), (0,)), ((), ())), preferred_element_type=jnp.float32)


def tn(a, b):
    return lax.dot_general(a, b, (((0,), (0,)), ((), ())), preferred_element_type=jnp.float32)


def kernel(
    chips,
    lists,
    q_hbm,
    k_hbm,
    v_hbm,
    g_hbm,
    dq_out,
    dk_out,
    dv_out,
    hand_out,
    own,
    near,
    mask_own,
    mask_chip,
    mask_near,
    e_buf,
    d_buf,
    stat_out,
    stat_own,
    stat_in,
    fac_out,
    fac_own,
    fac_in,
    dq_own,
    dq_send,
    dq_recv,
    stage,
    local_sem,
    part_send,
    part_recv,
    near_send,
    near_recv,
    mask_send,
    mask_recv,
    mask_part,
    stat_send,
    stat_recv,
    fac_send,
    fac_recv,
    dq_ssem,
    dq_rsem,
    out_send,
    out_recv,
    hand_send,
    hand_recv,
):
    section = lax.axis_index("section")
    me = lax.axis_index("ctx")
    chip = me // CORES
    core = lax.rem(me, CORES)
    other = 1 - core
    partner = CORES * chip + other
    below = lax.rem(chip + chips - 1, chips)
    above = lax.rem(chip + 1, chips)
    sides = (below, above)
    scale = DH ** (-0.5)
    inputs = (q_hbm, g_hbm, k_hbm, v_hbm)
    mine = pl.ds(pl.multiple_of(core * BLK, BLK), BLK)
    theirs = pl.ds(pl.multiple_of(other * BLK, BLK), BLK)

    def columns(half, slot):
        return pl.ds(pl.multiple_of((half * SLOTS + slot) * DH, DH), DH)

    def ctx(index):
        return {"ctx": index}

    def load_local(slot, carry):
        for n, ref in enumerate(inputs):
            pltpu.make_async_copy(
                ref.at[0, :, columns(core, slot)], own.at[slot, n, mine, :], local_sem.at[slot]
            ).start()
        return carry

    lax.fori_loop(0, SLOTS, load_local, 0)

    row = lax.broadcasted_iota(jnp.int32, (8, BLK), 0)
    flags = jnp.zeros((8, BLK), jnp.float32)
    for step in range(2 * REACH + 1):
        named = jnp.float32(0)
        for n in range(2 * REACH + 1):
            entry = lists[0, n]
            hit = (entry == me + (step - REACH)) & (entry >= 0)
            named = jnp.maximum(named, jnp.where(hit, jnp.float32(1), jnp.float32(0)))
        flags = jnp.where(row == step, named, flags)
    mask_own[...] = flags

    barrier = pltpu.get_barrier_semaphore()
    greet = [{"ctx": partner}]
    greet += [{"ctx": CORES * side + d} for side in sides for d in range(CORES)]
    greet += [{"section": 1 - section, "ctx": CORES * chip + d} for d in range(CORES)]
    for device in greet:
        pl.semaphore_signal(barrier, inc=1, device_id=device, device_id_type=MESH)
    pl.semaphore_wait(barrier, len(greet))

    def remote(src, dst, ssem, rsem, device):
        return pltpu.make_async_remote_copy(
            src_ref=src, dst_ref=dst, send_sem=ssem, recv_sem=rsem, device_id=device, device_id_type=MESH
        )

    def arrived(ref, sem):
        pltpu.make_async_copy(ref, ref, sem).wait()

    for side in range(2):
        for d in range(CORES):
            remote(
                mask_own, mask_near.at[1 - side, core], mask_send.at[0], mask_recv.at[1 - side],
                ctx(CORES * sides[side] + d),
            ).start()
    remote(mask_own, mask_chip.at[core], mask_part.at[0], mask_part.at[1], ctx(partner)).start()
    mask_chip[core] = flags

    def send_near(slot):
        for side in range(2):
            for d in range(CORES):
                for n in range(2):
                    remote(
                        inputs[n].at[0, :, columns(d, slot)],
                        near.at[slot, 1 - side, n, mine, :],
                        near_send.at[slot],
                        near_recv.at[slot, 1 - side],
                        ctx(CORES * sides[side] + d),
                    ).start()

    def send_partner(slot):
        for n, ref in enumerate(inputs):
            remote(
                ref.at[0, :, columns(other, slot)],
                own.at[slot, n, mine, :],
                part_send.at[slot],
                part_recv.at[slot],
                ctx(partner),
            ).start()

    for slot in range(AHEAD):
        send_partner(slot)
        send_near(slot)
    for slot in range(AHEAD, SLOTS):
        send_partner(slot)

    @pl.when(section == 1)
    def _():
        hand_out[...] = jnp.zeros_like(hand_out)

    arrived(mask_near.at[0], mask_recv.at[0])
    arrived(mask_near.at[1], mask_recv.at[1])
    arrived(mask_chip.at[other], mask_part.at[1])

    def wanted(group, kb):
        parts = []
        for qb in range(CORES):
            step = kb - qb + REACH + CORES * (1 - group)
            if 0 <= step <= 2 * REACH:
                tile = mask_chip[qb] if group == 1 else mask_near[group // 2, qb]
                parts.append(tile[step : step + 1])
            else:
                parts.append(jnp.zeros((1, BLK), jnp.float32))
        return jnp.concatenate(parts, axis=1)

    def rows_of(slot, group, n):
        return own[slot, n] if group == 1 else near[slot, group // 2, n]

    def pack(first, *rest):
        rows = [first, *rest]
        pad = jnp.zeros((8 - len(rows), ROWS), jnp.float32)
        return jnp.concatenate([*rows, pad], axis=0)

    def step1(slot):
        arrived(own.at[slot, :, mine, :], local_sem.at[slot])
        arrived(own.at[slot, :, theirs, :], part_recv.at[slot])
        arrived(near.at[slot, 0], near_recv.at[slot, 0])
        arrived(near.at[slot, 1], near_recv.at[slot, 1])
        keys = own[slot, 2]
        values = own[slot, 3]
        for group in (0, 2, 1):
            scores = nt(keys, rows_of(slot, group, 0)) * scale
            halves = [
                jnp.where(wanted(group, kb) > 0, scores[kb * BLK : (kb + 1) * BLK], NEG)
                for kb in range(CORES)
            ]
            scores = jnp.concatenate(halves, axis=0)
            highest = jnp.max(scores, axis=0, keepdims=True)
            weights = jnp.exp(scores - highest)
            grad_probs = nt(values, rows_of(slot, group, 1))
            total = jnp.sum(weights, axis=0, keepdims=True)
            cross = jnp.sum(weights * grad_probs, axis=0, keepdims=True)
            e_buf[slot, group] = weights
            d_buf[slot, group] = grad_probs
            tile = pack(highest, total, cross)
            if group == 1:
                stat_own[slot] = tile
            else:
                side = group // 2
                stat_out[slot, side] = tile
                remote(
                    stat_out.at[slot, side], stat_in.at[slot, 1 - side],
                    stat_send.at[slot, side], stat_recv.at[slot, 1 - side],
                    ctx(CORES * sides[side] + core),
                ).start()

    def combine(slot):
        for side in range(2):
            arrived(stat_in.at[slot, side], stat_recv.at[slot, side])
        tiles = [stat_in[slot, 0], stat_own[slot], stat_in[slot, 1]]
        highest = jnp.maximum(jnp.maximum(tiles[0][0:1], tiles[1][0:1]), tiles[2][0:1])
        shrink = [jnp.exp(tile[0:1] - highest) for tile in tiles]
        denom = sum(tile[1:2] * s for tile, s in zip(tiles, shrink))
        delta = sum(tile[2:3] * s for tile, s in zip(tiles, shrink)) / denom
        for side in range(2):
            fac_out[slot, side] = pack(shrink[2 * side] / denom, delta)
            remote(
                fac_out.at[slot, side], fac_in.at[slot, 1 - side],
                fac_send.at[slot, side], fac_recv.at[slot, 1 - side],
                ctx(CORES * sides[side] + core),
            ).start()
        fac_own[slot] = pack(shrink[1] / denom, delta)

    def step2(slot):
        for side in range(2):
            arrived(fac_in.at[slot, side], fac_recv.at[slot, side])
        keys = own[slot, 2]
        key_grad = jnp.zeros((ROWS, DH), jnp.float32)
        value_grad = jnp.zeros((ROWS, DH), jnp.float32)
        for group in (0, 2, 1):
            tile = fac_own[slot] if group == 1 else fac_in[slot, group // 2]
            probs = e_buf[slot, group] * tile[0:1]
            probs_low = probs.astype(jnp.bfloat16)
            scores_low = (probs * (d_buf[slot, group] - tile[1:2])).astype(jnp.bfloat16)
            query_grad = tn(keys, scores_low) * scale
            if group == 1:
                dq_own[slot] = query_grad
            else:
                side = group // 2
                dq_send[slot, side] = query_grad.astype(jnp.bfloat16)
                remote(
                    dq_send.at[slot, side], dq_recv.at[slot, 1 - side],
                    dq_ssem.at[slot, side], dq_rsem.at[slot, 1 - side],
                    ctx(CORES * sides[side] + core),
                ).start()
            value_grad = value_grad + nn(probs_low, rows_of(slot, group, 1))
            key_grad = key_grad + nn(scores_low, rows_of(slot, group, 0))
        stage[slot, 1] = (key_grad * scale).astype(jnp.bfloat16)
        stage[slot, 2] = value_grad.astype(jnp.bfloat16)

        @pl.when(section == 1)
        def _():
            for b in range(CORES):
                remote(
                    stage.at[slot, 2, b * BLK : (b + 1) * BLK, :],
                    hand_out.at[0, :, columns(core, slot)],
                    hand_send.at[0],
                    hand_recv.at[0],
                    {"section": section - 1, "ctx": CORES * chip + b},
                ).start()

        for n, out in ((1, dk_out), (2, dv_out)):
            deliver(slot, n, out)

    def deliver(slot, n, out):
        remote(
            stage.at[slot, n, theirs, :],
            out.at[0, :, columns(core, slot)],
            out_send.at[0],
            out_recv.at[0],
            ctx(partner),
        ).start()
        out[0, :, columns(core, slot)] = stage[slot, n, mine, :]

    def final(slot):
        for side in range(2):
            arrived(dq_recv.at[slot, side], dq_rsem.at[slot, side])
        total = (
            dq_own[slot] + dq_recv[slot, 0].astype(jnp.float32) + dq_recv[slot, 1].astype(jnp.float32)
        )
        stage[slot, 0] = jnp.transpose(total).astype(jnp.bfloat16)
        deliver(slot, 0, dq_out)

    def turn(i, carry):
        @pl.when(i < SLOTS)
        def _():
            step1(i)

        @pl.when(i + AHEAD < SLOTS)
        def _():
            send_near(i + AHEAD)

        @pl.when((i >= 1) & (i < SLOTS + 1))
        def _():
            combine(i - 1)

        @pl.when((i >= 2) & (i < SLOTS + 2))
        def _():
            step2(i - 2)

        @pl.when((i >= 3) & (i < SLOTS + 3))
        def _():
            final(i - 3)

        return carry

    lax.fori_loop(0, SLOTS + 3, turn, 0)

    arrived(mask_near, mask_send.at[0])
    arrived(mask_own, mask_part.at[0])

    def drain(slot, carry):
        arrived(own.at[slot], near_send.at[slot])
        arrived(near.at[slot, 0], part_send.at[slot])
        for side in range(2):
            arrived(stat_out.at[slot, side], stat_send.at[slot, side])
            arrived(fac_out.at[slot, side], fac_send.at[slot, side])
            arrived(dq_send.at[slot, side], dq_ssem.at[slot, side])
        return carry

    lax.fori_loop(0, SLOTS, drain, 0)
    arrived(stage.at[:, :, mine, :], out_send.at[0])
    arrived(stage.at[:, :, mine, :], out_recv.at[0])

    @pl.when(section == 1)
    def _():
        arrived(hand_out, hand_send.at[0])

    @pl.when(section == 0)
    def _():
        arrived(hand_out, hand_recv.at[0])


def shards(query_rows, key_rows, value_rows, grad_output, block_lists):
    chips = lax.axis_size("ctx") // CORES
    shape = query_rows.shape
    low = jnp.bfloat16
    full = jnp.float32
    dma = pltpu.SemaphoreType.DMA
    any_spec = pl.BlockSpec(memory_space=pl.ANY)
    vmem_spec = pl.BlockSpec(memory_space=pltpu.VMEM)
    return pl.pallas_call(
        functools.partial(kernel, chips),
        out_shape=tuple(jax.ShapeDtypeStruct(shape, low) for _ in range(4)),
        in_specs=[pl.BlockSpec(memory_space=pltpu.SMEM)] + [any_spec] * 4,
        out_specs=tuple(vmem_spec for _ in range(4)),
        scratch_shapes=[
            pltpu.VMEM((SLOTS, 4, ROWS, DH), low),
            pltpu.VMEM((SLOTS, 2, 2, ROWS, DH), low),
            pltpu.VMEM((8, BLK), full),
            pltpu.VMEM((CORES, 8, BLK), full),
            pltpu.VMEM((2, CORES, 8, BLK), full),
            pltpu.VMEM((SLOTS, 3, ROWS, ROWS), full),
            pltpu.VMEM((SLOTS, 3, ROWS, ROWS), full),
            pltpu.VMEM((SLOTS, 2, 8, ROWS), full),
            pltpu.VMEM((SLOTS, 8, ROWS), full),
            pltpu.VMEM((SLOTS, 2, 8, ROWS), full),
            pltpu.VMEM((SLOTS, 2, 8, ROWS), full),
            pltpu.VMEM((SLOTS, 8, ROWS), full),
            pltpu.VMEM((SLOTS, 2, 8, ROWS), full),
            pltpu.VMEM((SLOTS, DH, ROWS), full),
            pltpu.VMEM((SLOTS, 2, DH, ROWS), low),
            pltpu.VMEM((SLOTS, 2, DH, ROWS), low),
            pltpu.VMEM((SLOTS, 3, ROWS, DH), low),
            dma((SLOTS,)),
            dma((SLOTS,)),
            dma((SLOTS,)),
            dma((SLOTS,)),
            dma((SLOTS, 2)),
            dma((1,)),
            dma((2,)),
            dma((2,)),
            dma((SLOTS, 2)),
            dma((SLOTS, 2)),
            dma((SLOTS, 2)),
            dma((SLOTS, 2)),
            dma((SLOTS, 2)),
            dma((SLOTS, 2)),
            dma((1,)),
            dma((1,)),
            dma((1,)),
            dma((1,)),
        ],
        compiler_params=pltpu.CompilerParams(collective_id=0, has_side_effects=True),
        name="attention_backward",
    )(block_lists, query_rows, key_rows, value_rows, grad_output)


def solution(mesh):
    spec = P("section", "ctx", None)
    return jax.shard_map(
        shards,
        mesh=mesh,
        in_specs=(spec, spec, spec, spec, P("ctx", None)),
        out_specs=(spec, spec, spec, spec),
        check_vma=False,
    )
```

time: 126 us -> 71.6 us (0.57)
  the two profiles are of different devices: /device:TPU:4 before, /device:TPU:1 now
where the time goes in v1:
time: 71.6 us; the launch traced here: 71.4 us
  Pallas kernels  65.9 us (92%)
  local copies, waits for them, and re-layouts  4.84 us (7%)
    pallas_call x1, Pallas kernels, shards(): pl.pallas_call(functools.partial(kernel, chips), out_shape=tuple((jax.Sha...  65.9 us
    unnamed x10, local copies, waits for them, and re-layouts  4.84 us

profile of v1, /device:TPU:1, one launch (start us, length us, event | category | flops | bytes accessed | tf_op | source)
XLA Modules:
  0.0 71.4 jit_solution(10536638023810726742)
XLA Ops:
  0.6 65.9 %attention_backward.1 = (bf16[1,128,1536]{2,1,0:T(8,128)(2,1)}, bf16[1,128,1536]{2,1,0:T(8,128)(2,1)}, bf16[1,128,1536]{2,1,0:T(8,128)(2,1)}, bf16[1,128,1536]{2,1,0:T(8,128)(2,1)}) custom-call(s32[1,5]{1,0:T(1,128)} %lists.1, bf16[1,128,1536]{2,1,0:T(8,128)(2,1)} %q_hbm.1, bf16[1,128,1536]{2,1,0:T(8,128)(2,1)} %k_hbm.1, bf16[1,128,1536]{2,1,0:T(8,128)(2,1)} %v_hbm.1, ...), custom_call_target="tpu_custom_call" | custom-call | tf_op jit(solution)/shard_map/attention_backward/pallas_call | solution.py:369
  66.5 0.0 copy-start.2
  66.5 1.8 %copy.13 = bf16[1,128,1536]{2,1,0:T(8,128)(2,1)} copy(bf16[1,128,1536]{2,1,0:T(8,128)(2,1)} %get-tuple-element.8) | data formatting | bytes 786432
  68.3 0.0 copy-done.2
  68.3 0.0 copy-start.1
  68.3 0.7 %copy.14 = bf16[1,128,1536]{2,1,0:T(8,128)(2,1)} copy(bf16[1,128,1536]{2,1,0:T(8,128)(2,1)S(1)} %copy-done.2) | data formatting | bytes 786432
  69.1 0.4 copy-done.1
  69.5 0.0 copy-start
  69.5 0.7 %copy.15 = bf16[1,128,1536]{2,1,0:T(8,128)(2,1)} copy(bf16[1,128,1536]{2,1,0:T(8,128)(2,1)S(1)} %copy-done.1) | data formatting | bytes 786432
  70.2 0.4 copy-done
  70.6 0.7 %copy.16 = bf16[1,128,1536]{2,1,0:T(8,128)(2,1)} copy(bf16[1,128,1536]{2,1,0:T(8,128)(2,1)S(1)} %copy-done) | data formatting | bytes 786432
Async XLA Ops:
  66.5 1.8 %copy-start.2 = (bf16[1,128,1536]{2,1,0:T(8,128)(2,1)S(1)}, bf16[1,128,1536]{2,1,0:T(8,128)(2,1)}, u32[]{:S(2)}) copy-start(bf16[1,128,1536]{2,1,0:T(8,128)(2,1)} %get-tuple-element.9) | copy-start | bytes 1179652
  68.3 1.1 %copy-start.1 = (bf16[1,128,1536]{2,1,0:T(8,128)(2,1)S(1)}, bf16[1,128,1536]{2,1,0:T(8,128)(2,1)}, u32[]{:S(2)}) copy-start(bf16[1,128,1536]{2,1,0:T(8,128)(2,1)} %get-tuple-element.10) | copy-start | bytes 1179652
  69.5 1.1 %copy-start = (bf16[1,128,1536]{2,1,0:T(8,128)(2,1)S(1)}, bf16[1,128,1536]{2,1,0:T(8,128)(2,1)}, u32[]{:S(2)}) copy-start(bf16[1,128,1536]{2,1,0:T(8,128)(2,1)} %get-tuple-element.11) | copy-start | bytes 1179652
